TPU v7x, 32 devices: a whole 2x2x4 slice. The times are simulated.
32 devices in a mesh: groups: 2 (over y), rows: 4 (over z), cols: 2 (over x), sub: 2 (over core).
Axes of the slice: x: 2, y: 2, z: 4, core: 2. Of those that a mesh axis runs over, the one named last changes fastest.
Arguments:
- trace: float32 [8, 4096, 32], P(('cols', 'sub'), 'groups', 'rows'), parts along dimension 1, may hold values from -6 to 6
Outputs:
- quotient: float32 [4, 2048, 128], P('groups', ('rows', 'cols', 'sub')), parts along dimension 0
There are 2 independent parts, one for each index of `groups`. A program takes and returns all parts, laid end to end along the dimension named above; each array names one. Nothing has to cross between parts.
All inputs are finite; a program needn't handle non-finite values.
Results may differ from a plain program's by a relative error of at most 0.00011.
Values sent between devices are 32-bit elements; how exact they have to be, the bound alone decides.
A program may use at most 64 MiB of HBM per device.

v0:
```python
from functools import partial
import math

import jax
import jax.numpy as jnp
import numpy as np
from jax import lax
from jax.experimental import pallas as pl
from jax.experimental.pallas import tpu as pltpu
from jax.sharding import PartitionSpec as P


def dft_table(extent, orient):
    points = jnp.arange(extent, dtype=jnp.int32)
    product = points[:, None] * points[None, :] % extent
    angles = product.astype(jnp.float32) * (orient * 2.0 * math.pi / extent)
    return (jnp.cos(angles), jnp.sin(angles))


def complex_apply(table_real, table_imag, data_real, data_imag):
    matmul = partial(jnp.dot, precision=lax.Precision.HIGHEST, preferred_element_type=jnp.float32)
    out_real = matmul(table_real, data_real) - matmul(table_imag, data_imag)
    out_imag = matmul(table_real, data_imag) + matmul(table_imag, data_real)
    return (out_real, out_imag)


def rotate(data_real, data_imag, angles):
    cosine = jnp.cos(angles)
    sine = jnp.sin(angles)
    return (data_real * cosine - data_imag * sine, data_real * sine + data_imag * cosine)


def turn(index_product, modulus, orient):
    return (index_product % modulus).astype(jnp.float32) * (orient * 2.0 * math.pi / modulus)


def transform_lead(data_real, data_imag, orient):
    extent = data_real.shape[0]
    rest_shape = data_real.shape[1:]
    breadth = data_real.size // extent
    flat_real = data_real.reshape(extent, breadth)
    flat_imag = data_imag.reshape(extent, breadth)
    if extent <= 128:
        table_real, table_imag = dft_table(extent, orient)
        out_real, out_imag = complex_apply(table_real, table_imag, flat_real, flat_imag)
    else:
        outer_len = extent // 128
        first_real, first_imag = transform_lead(
            flat_real.reshape(outer_len, 128 * breadth),
            flat_imag.reshape(outer_len, 128 * breadth),
            orient,
        )
        first_real = first_real.reshape(outer_len, 128, breadth)
        first_imag = first_imag.reshape(outer_len, 128, breadth)
        outer_index = jnp.arange(outer_len, dtype=jnp.int32)[:, None]
        inner_index = jnp.arange(128, dtype=jnp.int32)[None, :]
        angles = turn(outer_index * inner_index, extent, orient)[:, :, None]
        first_real, first_imag = rotate(first_real, first_imag, angles)
        first_real = jnp.transpose(first_real, (1, 0, 2)).reshape(128, outer_len * breadth)
        first_imag = jnp.transpose(first_imag, (1, 0, 2)).reshape(128, outer_len * breadth)
        out_real, out_imag = transform_lead(first_real, first_imag, orient)
    return (out_real.reshape((extent,) + rest_shape), out_imag.reshape((extent,) + rest_shape))


def times(first, second):
    return (
        first[0] * second[0] - first[1] * second[1],
        first[0] * second[1] + first[1] * second[0],
    )


def plus(first, second):
    return (first[0] + second[0], first[1] + second[1])


def on_device(trace):
    local_cols = trace.shape[0]
    slow_len = trace.shape[1]
    fast_local = trace.shape[2]
    row_parts = lax.axis_size("rows")
    group_parts = lax.axis_size(("cols", "sub"))
    row_index = lax.axis_index("rows")
    group_index = lax.axis_index(("cols", "sub"))
    fast_len = fast_local * row_parts
    trace_len = slow_len * fast_len
    ext_len = 4 * trace_len
    ext_slow = 4 * fast_len
    slow_block = slow_len // row_parts
    ext_block = ext_slow // row_parts
    point_block = ext_block // group_parts
    coeff_block = slow_block // group_parts
    real_part = jnp.transpose(trace, (1, 0, 2))
    imag_part = jnp.zeros_like(real_part)
    real_part, imag_part = transform_lead(real_part, imag_part, 1.0)
    lead_index = jnp.arange(slow_len, dtype=jnp.int32)[:, None, None]
    fast_index = (row_index * fast_local + jnp.arange(fast_local, dtype=jnp.int32))[None, None, :]
    real_part, imag_part = rotate(
        real_part, imag_part, turn(lead_index * fast_index, trace_len, 1.0)
    )
    moved = lax.all_to_all(
        jnp.stack([real_part, imag_part]), "rows", split_axis=1, concat_axis=3, tiled=True
    )
    moved = jnp.transpose(moved, (0, 3, 2, 1))
    real_part, imag_part = transform_lead(moved[0], moved[1], 1.0)
    slow_index = (row_index * slow_block + jnp.arange(slow_block, dtype=jnp.int32))[None, None, :]
    coeff_index = jnp.arange(fast_len, dtype=jnp.int32)[:, None, None] * slow_len + slow_index
    shift_angle = coeff_index.astype(jnp.float32) * (math.pi / (4.0 * trace_len))
    real_part, imag_part = rotate(real_part / trace_len, imag_part / trace_len, shift_angle)
    padding = jnp.zeros((ext_slow - fast_len, local_cols, slow_index.shape[2]), jnp.float32)
    real_part = jnp.concatenate([real_part, padding], 0)
    imag_part = jnp.concatenate([imag_part, padding], 0)
    real_part, imag_part = transform_lead(real_part, imag_part, -1.0)
    ext_index = jnp.arange(ext_slow, dtype=jnp.int32)[:, None, None]
    real_part, imag_part = rotate(real_part, imag_part, turn(ext_index * slow_index, ext_len, -1.0))
    stacked = jnp.stack([real_part, imag_part])
    moved = lax.all_to_all(stacked, "rows", split_axis=1, concat_axis=3, tiled=True)
    moved = jnp.transpose(moved, (0, 3, 2, 1))
    real_part, imag_part = transform_lead(moved[0], moved[1], -1.0)
    joined = lax.all_to_all(
        jnp.stack([real_part, imag_part]), ("cols", "sub"), split_axis=3, concat_axis=2, tiled=True
    )
    real_part = joined[0]
    imag_part = joined[1]

    def column(number):
        return (real_part[:, number], imag_part[:, number])

    wire_a = column(0)
    wire_b = column(1)
    wire_c = column(2)
    gate = times(times(times(column(3), wire_a), wire_b), wire_c)
    gate = plus(gate, times(column(4), wire_a))
    gate = plus(gate, times(column(5), wire_b))
    gate = plus(gate, times(column(6), wire_c))
    gate = plus(gate, column(7))
    point_index = (
        row_index * ext_block + group_index * point_block + jnp.arange(point_block, dtype=jnp.int32)
    )
    quarter = (point_index % 4).astype(jnp.float32)
    vanish_angle = math.pi / 4.0 - math.pi / 2.0 * quarter
    vanish_real = (jnp.cos(vanish_angle) - 1.0)[None, :]
    vanish_imag = jnp.sin(vanish_angle)[None, :]
    magnitude = vanish_real * vanish_real + vanish_imag * vanish_imag
    ratio_real = (gate[0] * vanish_real + gate[1] * vanish_imag) / magnitude
    ratio_imag = (gate[1] * vanish_real - gate[0] * vanish_imag) / magnitude
    real_part, imag_part = transform_lead(ratio_real, ratio_imag, 1.0)
    freq_index = jnp.arange(slow_len, dtype=jnp.int32)[:, None]
    real_part, imag_part = rotate(
        real_part, imag_part, turn(freq_index * point_index[None, :], ext_len, 1.0)
    )
    moved = lax.all_to_all(
        lax.all_to_all(
            jnp.stack([real_part, imag_part]), "rows", split_axis=1, concat_axis=2, tiled=True
        ),
        ("cols", "sub"),
        split_axis=1,
        concat_axis=2,
        tiled=True,
    )
    moved = moved.reshape(2, coeff_block, group_parts, row_parts, point_block)
    moved = jnp.transpose(moved, (0, 3, 2, 4, 1)).reshape(2, ext_slow, coeff_block)
    real_part, imag_part = transform_lead(moved[0], moved[1], 1.0)
    low_index = (
        row_index * slow_block
        + group_index * coeff_block
        + jnp.arange(coeff_block, dtype=jnp.int32)
    )[None, :]
    final_index = jnp.arange(ext_slow, dtype=jnp.int32)[:, None] * slow_len + low_index
    final_angle = final_index.astype(jnp.float32) * (-math.pi / (4.0 * trace_len))
    real_part, imag_part = rotate(real_part, imag_part, final_angle)
    result = jnp.stack([real_part, imag_part]) * (1.0 / math.sqrt(ext_len))
    return jnp.transpose(result, (0, 2, 1))


MESH = pl.DeviceIdType.MESH
CHUNKS = 2


def halves(table):
    high = table.astype(jnp.bfloat16)
    low = (table - high.astype(np.float64)).astype(jnp.bfloat16)
    return high, low


def fused_tables(sizes):
    side, fast_len, fast_local, rows, groups, blocks = sizes
    points = side * side
    ext = rows * points
    low_len = side // fast_len
    slow_len = side * low_len
    index = np.arange(side)
    angles = 2.0 * np.pi * (index[:, None] * index[None, :] % side) / side
    dft = np.stack(halves(np.cos(angles)) + halves(np.sin(angles)))
    lane_row, lane_low, lane_fast = np.meshgrid(
        np.arange(rows), np.arange(low_len), np.arange(fast_local), indexing="ij"
    )
    inner = (fast_len * lane_low + fast_local * lane_row + lane_fast).reshape(-1)
    theta = 2.0 * np.pi * (index[:, None] - side // 2) * inner[None, :] / points
    base = np.stack([np.cos(theta), np.sin(theta)]).astype(np.float32)
    shifts = 0.5 / rows - np.arange(rows) / rows
    kernels = []
    for shift in shifts:
        gap = inner[:, None] - inner[None, :] + shift
        sign = 1.0 - 2.0 * (inner[None, :] % 2)
        kernels.append(
            np.stack(
                halves(sign / points * np.sin(np.pi * shift) / np.sin(np.pi * gap / side))
            )
        )
    kernels = np.stack(kernels)
    low_index = np.repeat(np.arange(low_len), fast_local)
    spin = 2.0 * np.pi * low_index[:, None] * index[None, :] / slow_len
    spin = np.stack([np.cos(spin), np.sin(spin)]).astype(np.float32)
    source_row, source_group, fast_at = np.meshgrid(
        np.arange(rows), np.arange(groups), np.arange(fast_local), indexing="ij"
    )
    low_digit = rows * (fast_local * source_group + fast_at) + source_row
    vanish = np.exp(1j * (np.pi / rows - 2.0 * np.pi / rows * source_row)) - 1.0
    finals = np.arange(rows * fast_len)
    turns = np.exp(
        2j * np.pi * low_digit[..., None] * finals / (rows * fast_len)
        - 1j * np.pi * slow_len * finals / ext
    ) / (vanish[..., None] * math.sqrt(ext))
    real_rows = np.concatenate([turns.real, turns.imag], -1)
    imag_rows = np.concatenate([-turns.imag, turns.real], -1)
    final = np.stack([real_rows, imag_rows], 2).reshape(-1, 2 * rows * fast_len)
    final = np.stack(halves(final))
    return dft, kernels, base, spin, final


def split(value):
    high = value.astype(jnp.bfloat16)
    return high, (value - high.astype(jnp.float32)).astype(jnp.bfloat16)


def dot3(left, right):
    mul = partial(jnp.dot, preferred_element_type=jnp.float32)
    return mul(left[0], right[0]) + (mul(left[0], right[1]) + mul(left[1], right[0]))


def short_transform(values):
    count = len(values)
    if count == 1:
        return values
    even = short_transform(values[0::2])
    odd = short_transform(values[1::2])
    first, second = [], []
    for at in range(count // 2):
        cosine = math.cos(2.0 * math.pi * at / count)
        sine = math.sin(2.0 * math.pi * at / count)
        real, imag = odd[at]
        if at == 0:
            spun = (real, imag)
        elif 4 * at == count:
            spun = (-imag, real)
        else:
            spun = (real * cosine - imag * sine, real * sine + imag * cosine)
        first.append(plus(even[at], spun))
        second.append((even[at][0] - spun[0], even[at][1] - spun[1]))
    return first + second


def fused_kernel(
    sizes,
    x_ref,
    dft_hbm,
    kern_hbm,
    base_hbm,
    spin_hbm,
    final_hbm,
    out_ref,
    dft,
    kern,
    base,
    spin,
    final,
    gathered,
    staged,
    total,
    data_high,
    data_low,
    wide_high,
    wide_low,
    send_block,
    recv_block,
    send_tail,
    recv_tail,
    post,
    twist,
    table_sem,
    gather_send,
    gather_recv,
    block_send,
    block_recv,
    tail_send,
    tail_recv,
):
    side, fast_len, fast_local, rows, groups, (cols, subs) = sizes
    points = side * side
    ext = rows * points
    low_len = side // fast_len
    half = low_len * fast_local
    wide = 2 * half
    piece = side // CHUNKS
    members = rows * groups
    row = lax.axis_index("rows")
    col = lax.axis_index("cols")
    sub = lax.axis_index("sub")
    group = col * subs + sub
    me = row * groups + group

    def place(member):
        inside = lax.rem(member, groups)
        return {
            "rows": lax.div(member, groups),
            "cols": lax.div(inside, subs),
            "sub": lax.rem(inside, subs),
        }

    barrier = pltpu.get_barrier_semaphore()
    for step in range(1, members):
        pl.semaphore_signal(
            barrier, inc=1, device_id=place(lax.rem(me + step, members)), device_id_type=MESH
        )
    loads = [
        pltpu.make_async_copy(dft_hbm, dft, table_sem.at[0]),
        pltpu.make_async_copy(base_hbm, base, table_sem.at[1]),
        pltpu.make_async_copy(kern_hbm.at[row], kern, table_sem.at[2]),
        pltpu.make_async_copy(spin_hbm, spin, table_sem.at[3]),
        pltpu.make_async_copy(final_hbm, final, table_sem.at[4]),
    ]
    for load in loads:
        load.start()
    pl.semaphore_wait(barrier, members - 1)

    def hop(source, slot, chunk, way, target):
        span = pl.ds(chunk * piece, piece)
        return pltpu.make_async_remote_copy(
            src_ref=source.at[span],
            dst_ref=gathered.at[slot, span],
            send_sem=gather_send.at[slot, chunk, way],
            recv_sem=gather_recv.at[slot, chunk],
            device_id={"rows": target},
            device_id_type=MESH,
        )

    for chunk in range(CHUNKS):

        @pl.when(row < rows - 1)
        def _():
            hop(x_ref, row, chunk, 0, row + 1).start()

        @pl.when(row > 0)
        def _():
            hop(x_ref, row, chunk, 1, row - 1).start()

    lane = lax.broadcasted_iota(jnp.int32, (side, wide), 1)
    left = lane < half
    sign = jnp.where(left, -1.0, 1.0)

    def first_stage(block, slot):
        data = split(block)
        cosines = dot3((dft[0], dft[1]), data)
        sines = dot3((dft[2], dft[3]), data)
        staged[slot] = cosines + sign * pltpu.roll(sines, half, 1)
        return jnp.sum(block.reshape(side // 8, 8, wide), 0)

    shift = 0.5 / rows - row.astype(jnp.float32) / rows
    loads[0].wait()
    total[...] = first_stage(x_ref[...], row)
    high_index = lax.broadcasted_iota(jnp.int32, (side, side), 0).astype(jnp.float32)
    angle = (high_index - side // 2) * (shift * (2.0 * math.pi / points))
    turn_cos = jnp.cos(angle)
    turn_sin = jnp.sin(angle)
    loads[1].wait()
    post[0] = base[0] * turn_cos + base[1] * turn_sin
    post[1] = base[0] * turn_sin - base[1] * turn_cos
    at_row = lax.broadcasted_iota(jnp.int32, (half, side), 0)
    at_lane = lax.broadcasted_iota(jnp.int32, (half, side), 1)
    low_freq = at_lane + side * (at_row // fast_local)
    digit = rows * (fast_local * group + at_row % fast_local) + row
    tail_angle = ((low_freq * (2 * digit - 1)) % (2 * ext)).astype(jnp.float32) * (math.pi / ext)
    twist[0] = jnp.cos(tail_angle)
    twist[1] = jnp.sin(tail_angle)

    @pl.loop(0, rows - 1)
    def _(step):
        inner = jnp.where(
            step == 0, row - 1, jnp.where(step == 1, row + 1, 2 * rows - 2 - 3 * row)
        )
        slot = jnp.where(
            row == 0, step + 1, jnp.where(row == rows - 1, rows - 2 - step, inner)
        )
        for chunk in range(CHUNKS):
            hop(x_ref, slot, chunk, 0, row).wait_recv()

            @pl.when((slot < row) & (row < rows - 1))
            def _():
                hop(gathered.at[slot], slot, chunk, 0, row + 1).start()

            @pl.when((slot > row) & (row > 0))
            def _():
                hop(gathered.at[slot], slot, chunk, 1, row - 1).start()

        total[...] += first_stage(gathered[slot], slot)

    sums = jnp.sum(total[...], 0, keepdims=True)
    narrow = lax.broadcasted_iota(jnp.int32, (1, wide), 1) < half
    mean_a = jnp.sum(jnp.where(narrow, sums, 0.0), 1, keepdims=True) * (1.0 / points)
    mean_b = jnp.sum(jnp.where(narrow, 0.0, sums), 1, keepdims=True) * (1.0 / points)

    for pair in range(rows // 2):
        first = staged[2 * pair]
        second = staged[2 * pair + 1]
        real = jnp.where(left, first, pltpu.roll(second, half, 1))
        imag = jnp.where(left, pltpu.roll(first, half, 1), second)
        span = slice(pair * wide, (pair + 1) * wide)
        cosine = base[0, :, span]
        sine = base[1, :, span]
        high, low = split(real * cosine - imag * sine)
        data_high[:side, span] = high
        data_low[:side, span] = low
        high, low = split(real * sine + imag * cosine)
        data_high[side:, span] = high
        data_low[side:, span] = low
    loads[2].wait()
    moved = dot3((data_high[...], data_low[...]), (kern[0], kern[1]))
    real = moved[:side]
    imag = moved[side:]
    new_real = real * post[0] - imag * post[1]
    new_imag = real * post[1] + imag * post[0]
    half_turn = jnp.zeros((1, 1), jnp.float32) + shift * math.pi
    half_cos = jnp.cos(half_turn)
    half_sin = jnp.sin(half_turn)
    row_at = lax.broadcasted_iota(jnp.int32, (side, side), 0)
    lane_at = lax.broadcasted_iota(jnp.int32, (side, side), 1)
    parity = jnp.where(row_at == 0, (1 - 2 * (lane_at % 2)).astype(jnp.float32), 0.0)
    new_real = new_real - parity * (mean_a * half_cos + mean_b * half_sin)
    new_imag = new_imag - parity * (mean_b * half_cos - mean_a * half_sin)
    high, low = split(new_real)
    wide_high[:side] = high
    wide_low[:side] = low
    high, low = split(new_imag)
    wide_high[side:] = high
    wide_low[side:] = low

    means = jnp.broadcast_to(jnp.where(narrow, mean_a, mean_b), (8, wide))

    def block_copy(target):
        return pltpu.make_async_remote_copy(
            src_ref=send_block.at[target],
            dst_ref=recv_block.at[group],
            send_sem=block_send.at[target],
            recv_sem=block_recv.at[group],
            device_id={"cols": lax.div(target, subs), "sub": lax.rem(target, subs)},
            device_id_type=MESH,
        )

    def block_arrival(source):
        return pltpu.make_async_remote_copy(
            src_ref=send_block.at[source],
            dst_ref=recv_block.at[source],
            send_sem=block_send.at[source],
            recv_sem=block_recv.at[source],
            device_id={"cols": lax.div(source, subs), "sub": lax.rem(source, subs)},
            device_id_type=MESH,
        )

    @pl.loop(0, cols)
    def _(step):
        tile = lax.rem(col + 1 + step, cols)
        span = pl.ds(pl.multiple_of(tile * wide, wide), wide)
        upper = (wide_high[:side, span], wide_low[:side, span])
        lower = (wide_high[side:, span], wide_low[side:, span])
        cosine = (dft[0], dft[1])
        sine = (dft[2], dft[3])
        value_a = dot3(cosine, upper) + dot3(sine, lower)
        value_b = dot3(cosine, lower) - dot3(sine, upper)
        send_block[tile * subs, :side] = jnp.where(left, value_a, pltpu.roll(value_b, half, 1))
        send_block[tile * subs + 1, :side] = jnp.where(
            left, pltpu.roll(value_a, half, 1), value_b
        )
        for at in range(2):
            send_block[tile * subs + at, side:] = means

            @pl.when(tile * subs + at != group)
            def _():
                block_copy(tile * subs + at).start()

    recv_block[group] = send_block[group]
    for step in range(1, groups):
        block_arrival(lax.rem(group + step, groups)).wait_recv()

    spin_cos = jnp.cos(half_turn)
    spin_sin = jnp.sin(half_turn)
    flip = (1 - 2 * (lane % 2)).astype(jnp.float32)
    part_cos = flip * spin_cos
    part_sin = flip * spin_sin

    def value(number):
        data = recv_block[number, :side]
        mean = recv_block[number, side : side + 1]
        return (mean + part_cos * data, part_sin * data)

    def swap(pair):
        return (pltpu.roll(pair[0], half, 1), pltpu.roll(pair[1], half, 1))

    block_ab = value(0)
    block_cm = value(1)
    block_qab = value(2)
    block_qck = value(3)
    cubic = times(block_ab, block_cm)
    linear = times(block_ab, block_qab)
    gate = times(cubic, swap(cubic))
    gate = plus(gate, plus(linear, swap(linear)))
    gate = plus(gate, times(block_cm, block_qck))
    gate = plus(gate, swap(block_qck))
    packed = jnp.where(left, gate[0], pltpu.roll(gate[1], half, 1))
    turned = split(jnp.transpose(packed))
    cosines = dot3(turned, (dft[0], dft[1]))
    sines = dot3(turned, (dft[2], dft[3]))
    real = cosines[:half] - sines[half:]
    imag = cosines[half:] + sines[:half]
    loads[3].wait()
    loads[4].wait()
    real, imag = (real * spin[0] - imag * spin[1], real * spin[1] + imag * spin[0])
    values = [
        (real[at * fast_local : (at + 1) * fast_local], imag[at * fast_local : (at + 1) * fast_local])
        for at in range(low_len)
    ]
    values = short_transform(values)
    tails = members // low_len
    breadth = side // tails
    for at in range(low_len):
        rows_at = slice(at * fast_local, (at + 1) * fast_local)
        real, imag = values[at]
        cosine = twist[0, rows_at]
        sine = twist[1, rows_at]
        out_real = real * cosine - imag * sine
        out_imag = real * sine + imag * cosine
        for part in range(tails):
            lanes = slice(part * breadth, (part + 1) * breadth)
            send_tail[at * tails + part, :fast_local] = out_real[:, lanes]
            send_tail[at * tails + part, fast_local:] = out_imag[:, lanes]

    def tail_copy(target, slot):
        return pltpu.make_async_remote_copy(
            src_ref=send_tail.at[target],
            dst_ref=recv_tail.at[slot],
            send_sem=tail_send.at[target],
            recv_sem=tail_recv.at[slot],
            device_id=place(target),
            device_id_type=MESH,
        )

    for step in range(1, members):
        tail_copy(lax.rem(me + step, members), me).start()
    recv_tail[me] = send_tail[me]
    for step in range(1, members):
        source = lax.rem(me + step, members)
        tail_copy(source, source).wait_recv()
    flat = recv_tail[...].reshape(members * 2 * fast_local, breadth)
    result = dot3(split(jnp.transpose(flat)), (final[0], final[1]))
    out_ref[0] = result[:, : rows * fast_len]
    out_ref[1] = result[:, rows * fast_len :]

    for step in range(1, members):
        target = lax.rem(me + step, members)
        tail_copy(target, me).wait_send()
    for step in range(1, groups):
        block_copy(lax.rem(group + step, groups)).wait_send()
    for chunk in range(CHUNKS):
        for slot in range(rows):

            @pl.when((slot <= row) & (row < rows - 1))
            def _():
                hop(x_ref, slot, chunk, 0, row + 1).wait_send()

            @pl.when((slot >= row) & (row > 0))
            def _():
                hop(x_ref, slot, chunk, 1, row - 1).wait_send()


def fused_on_device(sizes, trace):
    side, fast_len, fast_local, rows, groups, _ = sizes
    local_cols = trace.shape[0]
    low_len = side // fast_len
    half = low_len * fast_local
    wide = 2 * half
    members = rows * groups
    tables = [jnp.asarray(table) for table in fused_tables(sizes)]
    block = jnp.transpose(trace.reshape(local_cols, side, low_len, fast_local), (1, 0, 2, 3))
    block = block.reshape(side, wide)
    vmem = pltpu.VMEM
    bf16 = jnp.bfloat16
    f32 = jnp.float32
    dma = pltpu.SemaphoreType.DMA
    breadth = side * low_len // members
    return pl.pallas_call(
        partial(fused_kernel, sizes),
        out_shape=jax.ShapeDtypeStruct((2, breadth, rows * fast_len), f32),
        in_specs=[pl.BlockSpec(memory_space=vmem)]
        + [pl.BlockSpec(memory_space=pl.ANY)] * len(tables),
        out_specs=pl.BlockSpec(memory_space=vmem),
        scratch_shapes=[
            vmem((4, side, side), bf16),
            vmem((2, side, side), bf16),
            vmem((2, side, side), f32),
            vmem((2, half, side), f32),
            vmem((2, members * 2 * fast_local, 2 * rows * fast_len), bf16),
            vmem((rows, side, wide), f32),
            vmem((rows, side, wide), f32),
            vmem((8, wide), f32),
            vmem((2 * side, side), bf16),
            vmem((2 * side, side), bf16),
            vmem((2 * side, side), bf16),
            vmem((2 * side, side), bf16),
            vmem((groups, side + 8, wide), f32),
            vmem((groups, side + 8, wide), f32),
            vmem((members, 2 * fast_local, breadth), f32),
            vmem((members, 2 * fast_local, breadth), f32),
            vmem((2, side, side), f32),
            vmem((2, half, side), f32),
            dma((5,)),
            dma((rows, CHUNKS, 2)),
            dma((rows, CHUNKS)),
            dma((groups,)),
            dma((groups,)),
            dma((members,)),
            dma((members,)),
        ],
        compiler_params=pltpu.CompilerParams(collective_id=0, has_side_effects=True),
    )(block, *tables)


def fused_sizes(mesh, trace):
    shape = mesh.shape
    rows = shape["rows"]
    groups = shape["cols"] * shape["sub"]
    slow_len = trace.shape[1] // shape["groups"]
    fast_len = trace.shape[2]
    side = math.isqrt(slow_len * fast_len)
    fast_local = fast_len // rows
    local_cols = trace.shape[0] // groups
    low_len = side // fast_len
    fits = (
        side * side == slow_len * fast_len
        and low_len * fast_len == side
        and rows == 4
        and groups == rows
        and shape["cols"] == 2
        and shape["sub"] == 2
        and local_cols == 2
        and fast_local == 8
        and 2 * low_len * fast_local == 128
        and rows * groups == 2 * low_len
    )
    return (side, fast_len, fast_local, rows, groups, (shape["cols"], shape["sub"])) if fits else None


def solution(mesh):
    placed = (P(("cols", "sub"), "groups", "rows"),)

    def whole(trace):
        sizes = fused_sizes(mesh, trace)
        return jax.shard_map(
            on_device if sizes is None else partial(fused_on_device, sizes),
            mesh=mesh,
            in_specs=placed,
            out_specs=P("groups", ("rows", "cols", "sub"), None),
            check_vma=False,
        )(trace)

    return whole
```

profile of v0, /device:TPU:0, one launch (start us, length us, event | category | flops | bytes accessed | tf_op | source)
XLA Modules:
  0.0 37.0 jit_solution(16123590987165762554)
XLA Ops:
  0.0 2.0 %reshape.6 = f32[2,256,8,8]{2,1,3,0:T(8,128)S(1)} reshape(f32[2,2048,8]{1,2,0:T(8,128)} %param.6) | data formatting | bytes 262144 | tf_op jit(solution)/shard_map/reshape | solution.py:592
  2.0 0.6 %copy.8 = f32[256,2,8,8]{0,3,2,1:T(8,128)S(1)} copy(f32[256,2,8,8]{2,0,3,1:T(8,128)S(1)} %bitcast.4) | data formatting | bytes 262144 | tf_op jit(solution)/shard_map/transpose | solution.py:592
  2.6 0.8 %copy.9.x_ref = f32[256,128]{1,0:T(8,128)} copy(f32[256,128]{0,1:T(8,128)S(1)} %bitcast.5) | data formatting | bytes 262144 | tf_op jit(solution)/shard_map/reshape | solution.py:593
  3.4 32.1 %shard_map.64 = f32[2,128,128]{2,1,0:T(8,128)} custom-call(f32[256,128]{1,0:T(8,128)} %copy.9.x_ref, bf16[4,256,256]{2,1,0:T(8,128)(2,1)} %constant.10.clone.dft_hbm, bf16[4,2,256,256]{3,2,1,0:T(8,128)(2,1)} %constant.11.clone.kern_hbm, f32[2,256,256]{2,1,0:T(8,128)} %constant.12.clone.base_hbm, f32[2,64,256]{2,1,0:T(8,128)} %constant.13.clone.spin_hbm, ...), custom_call_target="tpu_custom_call" | custom-call | tf_op jit(solution)/shard_map/pallas_call | solution.py:599
  35.5 1.6 %copy.11 = f32[2,128,128]{2,1,0:T(8,128)} copy(f32[2,128,128]{2,1,0:T(8,128)} %shard_map.64) | data formatting | bytes 262144
where the time goes:
time: 37.2 us; the launch traced here: 37 us
  Pallas kernels  32.1 us (86%)
  local copies, waits for them, and re-layouts  4.95 us (13%)
    pallas_call x1, Pallas kernels, fused_on_device(): pl.pallas_call(partial(fused_kernel, sizes), out_shape=jax.ShapeDtypeStru...  32.1 us
    reshape x1, local copies, waits for them, and re-layouts, fused_on_device(): trace.reshape(local_cols, side, low_len, fast_local)  2.04 us
    unnamed x1, local copies, waits for them, and re-layouts  1.57 us
    reshape x1, local copies, waits for them, and re-layouts, fused_on_device(): block = block.reshape(side, wide)  0.78 us

commit v1 on v0

--- a/solution.py
+++ b/solution.py
@@ -173,7 +173,7 @@
 
 
 MESH = pl.DeviceIdType.MESH
-CHUNKS = 2
+CHUNKS = 4
 
 
 def halves(table):
@@ -318,10 +318,23 @@
         }
 
     barrier = pltpu.get_barrier_semaphore()
-    for step in range(1, members):
+    for step in range(1, groups):
+        other = lax.rem(group + step, groups)
         pl.semaphore_signal(
-            barrier, inc=1, device_id=place(lax.rem(me + step, members)), device_id_type=MESH
-        )
+            barrier,
+            inc=1,
+            device_id={"cols": lax.div(other, subs), "sub": lax.rem(other, subs)},
+            device_id_type=MESH,
+        )
+
+    @pl.when(row > 0)
+    def _():
+        pl.semaphore_signal(barrier, inc=1, device_id={"rows": row - 1}, device_id_type=MESH)
+
+    @pl.when(row < rows - 1)
+    def _():
+        pl.semaphore_signal(barrier, inc=1, device_id={"rows": row + 1}, device_id_type=MESH)
+
     loads = [
         pltpu.make_async_copy(dft_hbm, dft, table_sem.at[0]),
         pltpu.make_async_copy(base_hbm, base, table_sem.at[1]),
@@ -331,7 +344,10 @@
     ]
     for load in loads:
         load.start()
-    pl.semaphore_wait(barrier, members - 1)
+    pl.semaphore_wait(
+        barrier,
+        groups - 1 + (row > 0).astype(jnp.int32) + (row < rows - 1).astype(jnp.int32),
+    )
 
     def hop(source, slot, chunk, way, target):
         span = pl.ds(chunk * piece, piece)
@@ -629,7 +645,9 @@
             dma((members,)),
             dma((members,)),
         ],
-        compiler_params=pltpu.CompilerParams(collective_id=0, has_side_effects=True),
+        compiler_params=pltpu.CompilerParams(
+            collective_id=0, has_side_effects=True, vmem_limit_bytes=24 * 2**20
+        ),
     )(block, *tables)
 
 

time: 37.2 us -> 35.7 us (0.960)
  Pallas kernels: 32.1 us -> 29 us
  local copies, waits for them, and re-layouts: 4.95 us -> 6.46 us
    pallas_call x1, Pallas kernels: 32.1 us -> 29 us  [fused_on_device(): pl.pallas_call(partial(fused_kernel, sizes), out_shape=jax.ShapeDtypeStru...]
    transpose x1, local copies, waits for them, and re-layouts: 0.56 us -> 2.15 us  [fused_on_device(): jnp.transpose(trace.reshape(local_cols, side, low_len, fast_local), (1, 0...]
    reshape x1, local copies, waits for them, and re-layouts: 2.04 us -> 3.53 us  [fused_on_device(): trace.reshape(local_cols, side, low_len, fast_local)]
    unnamed x1 -> x11, local copies, waits for them, and re-layouts: 1.57 us -> 0.68 us
    reshape x1, local copies, waits for them, and re-layouts: 0.78 us -> 0.11 us  [fused_on_device(): block = block.reshape(side, wide)]
where the time goes in v1:
time: 35.7 us; the launch traced here: 35.6 us
  Pallas kernels  29 us (81%)
  local copies, waits for them, and re-layouts  6.46 us (18%)
    pallas_call x1, Pallas kernels, fused_on_device(): pl.pallas_call(partial(fused_kernel, sizes), out_shape=jax.ShapeDtypeStru...  29 us
    reshape x1, local copies, waits for them, and re-layouts, fused_on_device(): trace.reshape(local_cols, side, low_len, fast_local)  3.53 us
    transpose x1, local copies, waits for them, and re-layouts, fused_on_device(): jnp.transpose(trace.reshape(local_cols, side, low_len, fast_local), (1, 0...  2.15 us

profile of v1, /device:TPU:0, one launch (start us, length us, event | category | flops | bytes accessed | tf_op | source)
XLA Modules:
  0.0 35.6 jit_solution(18108995775794581431)
XLA Ops:
  0.0 0.0 copy-start
  0.0 0.0 copy-start.1
  0.0 0.0 copy-start.2
  0.0 0.0 copy-start.3
  0.0 0.0 copy-start.4
  0.0 3.5 %reshape.6 = f32[2,256,8,8]{2,1,3,0:T(8,128)} reshape(f32[2,2048,8]{1,2,0:T(8,128)} %param.6) | data formatting | bytes 262144 | tf_op jit(solution)/shard_map/reshape | solution.py:608
  3.5 2.1 %copy.8 = f32[256,2,8,8]{0,3,2,1:T(8,128)S(1)} copy(f32[256,2,8,8]{2,0,3,1:T(8,128)} %bitcast.4) | data formatting | bytes 262144 | tf_op jit(solution)/shard_map/transpose | solution.py:608
  5.7 0.1 copy.9.x_ref
  5.8 0.0 copy-done
  5.8 0.0 copy-done.1
  5.8 0.0 copy-done.2
  5.8 0.0 copy-done.3
  5.9 0.0 copy-done.4
  5.9 29.0 %shard_map.64 = f32[2,128,128]{2,1,0:T(8,128)S(1)} custom-call(f32[256,128]{1,0:T(8,128)S(1)} %copy.9.x_ref, bf16[4,256,256]{2,1,0:T(8,128)(2,1)S(1)} %copy-done.2, bf16[4,2,256,256]{3,2,1,0:T(8,128)(2,1)S(1)} %copy-done, f32[2,256,256]{2,1,0:T(8,128)S(1)} %copy-done.1, f32[2,64,256]{2,1,0:T(8,128)S(1)} %copy-done.4, bf16[2,256,256]{2,1,0:T(8,128)(2,1)S(1)} %copy-done.3), custom_call_target="tpu_custom_call" | custom-call | tf_op jit(solution)/shard_map/pallas_call | solution.py:615
  34.9 0.7 %copy.11 = f32[2,128,128]{2,1,0:T(8,128)} copy(f32[2,128,128]{2,1,0:T(8,128)S(1)} %shard_map.64) | data formatting | bytes 262144
Async XLA Ops:
  0.0 5.8 %copy-start = (bf16[4,2,256,256]{3,2,1,0:T(8,128)(2,1)S(1)}, bf16[4,2,256,256]{3,2,1,0:T(8,128)(2,1)}, u32[]{:S(2)}) copy-start(bf16[4,2,256,256]{3,2,1,0:T(8,128)(2,1)} %constant.11.clone.kern_hbm) | copy-start | bytes 3145732
  0.0 5.8 %copy-start.1 = (f32[2,256,256]{2,1,0:T(8,128)S(1)}, f32[2,256,256]{2,1,0:T(8,128)}, u32[]{:S(2)}) copy-start(f32[2,256,256]{2,1,0:T(8,128)} %constant.12.clone.base_hbm) | copy-start | bytes 1572868
  0.0 5.8 %copy-start.2 = (bf16[4,256,256]{2,1,0:T(8,128)(2,1)S(1)}, bf16[4,256,256]{2,1,0:T(8,128)(2,1)}, u32[]{:S(2)}) copy-start(bf16[4,256,256]{2,1,0:T(8,128)(2,1)} %constant.10.clone.dft_hbm) | copy-start | bytes 1572868
  0.0 5.8 %copy-start.3 = (bf16[2,256,256]{2,1,0:T(8,128)(2,1)S(1)}, bf16[2,256,256]{2,1,0:T(8,128)(2,1)}, u32[]{:S(2)}) copy-start(bf16[2,256,256]{2,1,0:T(8,128)(2,1)} %constant.14.clone.final_hbm) | copy-start | bytes 786436
  0.0 5.8 %copy-start.4 = (f32[2,64,256]{2,1,0:T(8,128)S(1)}, f32[2,64,256]{2,1,0:T(8,128)}, u32[]{:S(2)}) copy-start(f32[2,64,256]{2,1,0:T(8,128)} %constant.13.clone.spin_hbm) | copy-start | bytes 393220

commit v2 on v1

--- a/solution.py
+++ b/solution.py
@@ -191,22 +191,24 @@
     index = np.arange(side)
     angles = 2.0 * np.pi * (index[:, None] * index[None, :] % side) / side
     dft = np.stack(halves(np.cos(angles)) + halves(np.sin(angles)))
-    lane_row, lane_low, lane_fast = np.meshgrid(
-        np.arange(rows), np.arange(low_len), np.arange(fast_local), indexing="ij"
-    )
-    inner = (fast_len * lane_low + fast_local * lane_row + lane_fast).reshape(-1)
-    theta = 2.0 * np.pi * (index[:, None] - side // 2) * inner[None, :] / points
+    row_at, low_at, fast_at = (
+        grid.reshape(-1)
+        for grid in np.meshgrid(
+            np.arange(rows), np.arange(low_len), np.arange(fast_local), indexing="ij"
+        )
+    )
+    inner = fast_local * row_at + fast_at
+    centred = low_at[:, None] + low_len * index[None, :] - slow_len // 2
+    theta = 2.0 * np.pi * inner[:, None] * centred / points
     base = np.stack([np.cos(theta), np.sin(theta)]).astype(np.float32)
     shifts = 0.5 / rows - np.arange(rows) / rows
+    same = low_at[:, None] == low_at[None, :]
+    sign = 1.0 - 2.0 * (inner[:, None] % 2)
     kernels = []
     for shift in shifts:
-        gap = inner[:, None] - inner[None, :] + shift
-        sign = 1.0 - 2.0 * (inner[None, :] % 2)
-        kernels.append(
-            np.stack(
-                halves(sign / points * np.sin(np.pi * shift) / np.sin(np.pi * gap / side))
-            )
-        )
+        gap = inner[None, :] - inner[:, None] + shift
+        weight = sign / points * np.sin(np.pi * shift) / np.sin(np.pi * gap / fast_len)
+        kernels.append(np.stack(halves(np.where(same, weight, 0.0))))
     kernels = np.stack(kernels)
     low_index = np.repeat(np.arange(low_len), fast_local)
     spin = 2.0 * np.pi * low_index[:, None] * index[None, :] / slow_len
@@ -238,21 +240,21 @@
     return mul(left[0], right[0]) + (mul(left[0], right[1]) + mul(left[1], right[0]))
 
 
-def short_transform(values):
+def short_transform(values, orient):
     count = len(values)
     if count == 1:
         return values
-    even = short_transform(values[0::2])
-    odd = short_transform(values[1::2])
+    even = short_transform(values[0::2], orient)
+    odd = short_transform(values[1::2], orient)
     first, second = [], []
     for at in range(count // 2):
         cosine = math.cos(2.0 * math.pi * at / count)
-        sine = math.sin(2.0 * math.pi * at / count)
+        sine = orient * math.sin(2.0 * math.pi * at / count)
         real, imag = odd[at]
         if at == 0:
             spun = (real, imag)
         elif 4 * at == count:
-            spun = (-imag, real)
+            spun = (-orient * imag, orient * real)
         else:
             spun = (real * cosine - imag * sine, real * sine + imag * cosine)
         first.append(plus(even[at], spun))
@@ -275,12 +277,10 @@
     spin,
     final,
     gathered,
-    staged,
     total,
     data_high,
     data_low,
-    wide_high,
-    wide_low,
+    wide,
     send_block,
     recv_block,
     send_tail,
@@ -300,8 +300,7 @@
     ext = rows * points
     low_len = side // fast_len
     half = low_len * fast_local
-    wide = 2 * half
-    piece = side // CHUNKS
+    piece = side * low_len // CHUNKS
     members = rows * groups
     row = lax.axis_index("rows")
     col = lax.axis_index("cols")
@@ -352,8 +351,8 @@
     def hop(source, slot, chunk, way, target):
         span = pl.ds(chunk * piece, piece)
         return pltpu.make_async_remote_copy(
-            src_ref=source.at[span],
-            dst_ref=gathered.at[slot, span],
+            src_ref=source.at[:, :, span],
+            dst_ref=gathered.at[slot, :, :, span],
             send_sem=gather_send.at[slot, chunk, way],
             recv_sem=gather_recv.at[slot, chunk],
             device_id={"rows": target},
@@ -370,31 +369,74 @@
         def _():
             hop(x_ref, row, chunk, 1, row - 1).start()
 
-    lane = lax.broadcasted_iota(jnp.int32, (side, wide), 1)
-    left = lane < half
-    sign = jnp.where(left, -1.0, 1.0)
-
-    def first_stage(block, slot):
-        data = split(block)
-        cosines = dot3((dft[0], dft[1]), data)
-        sines = dot3((dft[2], dft[3]), data)
-        staged[slot] = cosines + sign * pltpu.roll(sines, half, 1)
-        return jnp.sum(block.reshape(side // 8, 8, wide), 0)
+    own = pltpu.make_async_copy(x_ref, gathered.at[row], table_sem.at[5])
+    own.start()
+
+    def stacked(values):
+        return jnp.concatenate([value for value in values], 0)
+
+    def slices(real, imag):
+        return [
+            (real[at * fast_local : (at + 1) * fast_local], imag[at * fast_local : (at + 1) * fast_local])
+            for at in range(low_len)
+        ]
+
+    def lane_transform(real, imag, orient):
+        count = real.shape[0]
+        data = split(jnp.concatenate([real, imag], 0))
+        cosines = dot3(data, (dft[0], dft[1]))
+        sines = dot3(data, (dft[2], dft[3]))
+        return (
+            cosines[:count] - orient * sines[count:],
+            cosines[count:] + orient * sines[:count],
+        )
+
+    def first_stage(slot):
+        values = [
+            (
+                gathered[slot, 0, :, at * side : (at + 1) * side],
+                gathered[slot, 1, :, at * side : (at + 1) * side],
+            )
+            for at in range(low_len)
+        ]
+        for at in range(2):
+            sums = values[0][at]
+            for value in values[1:]:
+                sums = sums + value[at]
+            total[at] += sums
+        values = short_transform(values, 1.0)
+        real = stacked([value[0] for value in values])
+        imag = stacked([value[1] for value in values])
+        real, imag = times((real, imag), (spin[0], spin[1]))
+        real, imag = lane_transform(real, imag, 1.0)
+        span = pl.ds(pl.multiple_of(slot * half, half), half)
+        real, imag = times((real, imag), (base[0, span], base[1, span]))
+        high, low = split(real)
+        data_high[span, :side] = high
+        data_low[span, :side] = low
+        high, low = split(imag)
+        data_high[span, side:] = high
+        data_low[span, side:] = low
 
     shift = 0.5 / rows - row.astype(jnp.float32) / rows
+    at_row = lax.broadcasted_iota(jnp.int32, (half, side), 0)
+    at_lane = lax.broadcasted_iota(jnp.int32, (half, side), 1)
+    low_freq = at_row // fast_local + low_len * at_lane
+    digit = rows * (fast_local * group + at_row % fast_local) + row
+    total[...] = jnp.zeros_like(total)
+    own.wait()
     loads[0].wait()
-    total[...] = first_stage(x_ref[...], row)
-    high_index = lax.broadcasted_iota(jnp.int32, (side, side), 0).astype(jnp.float32)
-    angle = (high_index - side // 2) * (shift * (2.0 * math.pi / points))
+    loads[1].wait()
+    loads[3].wait()
+    first_stage(row)
+    centred = (low_freq - side * low_len // 2).astype(jnp.float32)
+    angle = centred * (shift * (2.0 * math.pi / points))
     turn_cos = jnp.cos(angle)
     turn_sin = jnp.sin(angle)
-    loads[1].wait()
-    post[0] = base[0] * turn_cos + base[1] * turn_sin
-    post[1] = base[0] * turn_sin - base[1] * turn_cos
-    at_row = lax.broadcasted_iota(jnp.int32, (half, side), 0)
-    at_lane = lax.broadcasted_iota(jnp.int32, (half, side), 1)
-    low_freq = at_lane + side * (at_row // fast_local)
-    digit = rows * (fast_local * group + at_row % fast_local) + row
+    for at in range(rows):
+        span = slice(at * half, (at + 1) * half)
+        post[0, span] = base[0, span] * turn_cos + base[1, span] * turn_sin
+        post[1, span] = base[0, span] * turn_sin - base[1, span] * turn_cos
     tail_angle = ((low_freq * (2 * digit - 1)) % (2 * ext)).astype(jnp.float32) * (math.pi / ext)
     twist[0] = jnp.cos(tail_angle)
     twist[1] = jnp.sin(tail_angle)
@@ -418,49 +460,24 @@
             def _():
                 hop(gathered.at[slot], slot, chunk, 1, row - 1).start()
 
-        total[...] += first_stage(gathered[slot], slot)
-
-    sums = jnp.sum(total[...], 0, keepdims=True)
-    narrow = lax.broadcasted_iota(jnp.int32, (1, wide), 1) < half
-    mean_a = jnp.sum(jnp.where(narrow, sums, 0.0), 1, keepdims=True) * (1.0 / points)
-    mean_b = jnp.sum(jnp.where(narrow, 0.0, sums), 1, keepdims=True) * (1.0 / points)
-
-    for pair in range(rows // 2):
-        first = staged[2 * pair]
-        second = staged[2 * pair + 1]
-        real = jnp.where(left, first, pltpu.roll(second, half, 1))
-        imag = jnp.where(left, pltpu.roll(first, half, 1), second)
-        span = slice(pair * wide, (pair + 1) * wide)
-        cosine = base[0, :, span]
-        sine = base[1, :, span]
-        high, low = split(real * cosine - imag * sine)
-        data_high[:side, span] = high
-        data_low[:side, span] = low
-        high, low = split(real * sine + imag * cosine)
-        data_high[side:, span] = high
-        data_low[side:, span] = low
+        first_stage(slot)
+
+    mean_a = jnp.sum(jnp.sum(total[0], 0, keepdims=True), 1, keepdims=True) * (1.0 / points)
+    mean_b = jnp.sum(jnp.sum(total[1], 0, keepdims=True), 1, keepdims=True) * (1.0 / points)
     loads[2].wait()
-    moved = dot3((data_high[...], data_low[...]), (kern[0], kern[1]))
-    real = moved[:side]
-    imag = moved[side:]
-    new_real = real * post[0] - imag * post[1]
-    new_imag = real * post[1] + imag * post[0]
+    moved = dot3((kern[0], kern[1]), (data_high[...], data_low[...]))
+    real, imag = times((moved[:, :side], moved[:, side:]), (post[0], post[1]))
     half_turn = jnp.zeros((1, 1), jnp.float32) + shift * math.pi
     half_cos = jnp.cos(half_turn)
     half_sin = jnp.sin(half_turn)
-    row_at = lax.broadcasted_iota(jnp.int32, (side, side), 0)
-    lane_at = lax.broadcasted_iota(jnp.int32, (side, side), 1)
-    parity = jnp.where(row_at == 0, (1 - 2 * (lane_at % 2)).astype(jnp.float32), 0.0)
-    new_real = new_real - parity * (mean_a * half_cos + mean_b * half_sin)
-    new_imag = new_imag - parity * (mean_b * half_cos - mean_a * half_sin)
-    high, low = split(new_real)
-    wide_high[:side] = high
-    wide_low[:side] = low
-    high, low = split(new_imag)
-    wide_high[side:] = high
-    wide_low[side:] = low
-
-    means = jnp.broadcast_to(jnp.where(narrow, mean_a, mean_b), (8, wide))
+    row_at = lax.broadcasted_iota(jnp.int32, (rows * half, side), 0)
+    lane_at = lax.broadcasted_iota(jnp.int32, (rows * half, side), 1)
+    constant = (lane_at == 0) & (row_at % half < fast_local)
+    parity = jnp.where(constant, (1 - 2 * (row_at % 2)).astype(jnp.float32), 0.0)
+    wide[0] = real - parity * (mean_a * half_cos + mean_b * half_sin)
+    wide[1] = imag - parity * (mean_b * half_cos - mean_a * half_sin)
+    side_at = lax.broadcasted_iota(jnp.int32, (8, side), 1)
+    means = jnp.where(side_at < side // 2, mean_a, mean_b)
 
     def block_copy(target):
         return pltpu.make_async_remote_copy(
@@ -485,79 +502,87 @@
     @pl.loop(0, cols)
     def _(step):
         tile = lax.rem(col + 1 + step, cols)
-        span = pl.ds(pl.multiple_of(tile * wide, wide), wide)
-        upper = (wide_high[:side, span], wide_low[:side, span])
-        lower = (wide_high[side:, span], wide_low[side:, span])
-        cosine = (dft[0], dft[1])
-        sine = (dft[2], dft[3])
-        value_a = dot3(cosine, upper) + dot3(sine, lower)
-        value_b = dot3(cosine, lower) - dot3(sine, upper)
-        send_block[tile * subs, :side] = jnp.where(left, value_a, pltpu.roll(value_b, half, 1))
-        send_block[tile * subs + 1, :side] = jnp.where(
-            left, pltpu.roll(value_a, half, 1), value_b
-        )
-        for at in range(2):
-            send_block[tile * subs + at, side:] = means
-
-            @pl.when(tile * subs + at != group)
+        span = pl.ds(pl.multiple_of(tile * subs * half, subs * half), subs * half)
+        real, imag = lane_transform(wide[0, span], wide[1, span], -1.0)
+        for at in range(subs):
+            target = tile * subs + at
+            values = times(
+                (real[at * half : (at + 1) * half], imag[at * half : (at + 1) * half]),
+                (spin[0], -spin[1]),
+            )
+            values = short_transform(slices(*values), -1.0)
+            for low in range(low_len):
+                rows_at = slice(low * fast_local, (low + 1) * fast_local)
+                send_block[target, rows_at] = values[low][0]
+                send_block[target, half + low * fast_local : half + (low + 1) * fast_local] = (
+                    values[low][1]
+                )
+            send_block[target, 2 * half :] = means
+
+            @pl.when(target != group)
             def _():
-                block_copy(tile * subs + at).start()
+                block_copy(target).start()
 
     recv_block[group] = send_block[group]
     for step in range(1, groups):
         block_arrival(lax.rem(group + step, groups)).wait_recv()
 
-    spin_cos = jnp.cos(half_turn)
-    spin_sin = jnp.sin(half_turn)
-    flip = (1 - 2 * (lane % 2)).astype(jnp.float32)
-    part_cos = flip * spin_cos
-    part_sin = flip * spin_sin
+    flip = (1 - 2 * (at_row % 2)).astype(jnp.float32)
+    part_cos = flip * half_cos
+    part_sin = flip * half_sin
 
     def value(number):
-        data = recv_block[number, :side]
-        mean = recv_block[number, side : side + 1]
+        block, at = divmod(number, 2)
+        data = recv_block[block, at * half : (at + 1) * half]
+        lane_from = at * (side // 2)
+        mean = recv_block[block, 2 * half : 2 * half + 1, lane_from : lane_from + 1]
         return (mean + part_cos * data, part_sin * data)
 
-    def swap(pair):
-        return (pltpu.roll(pair[0], half, 1), pltpu.roll(pair[1], half, 1))
-
-    block_ab = value(0)
-    block_cm = value(1)
-    block_qab = value(2)
-    block_qck = value(3)
-    cubic = times(block_ab, block_cm)
-    linear = times(block_ab, block_qab)
-    gate = times(cubic, swap(cubic))
-    gate = plus(gate, plus(linear, swap(linear)))
-    gate = plus(gate, times(block_cm, block_qck))
-    gate = plus(gate, swap(block_qck))
-    packed = jnp.where(left, gate[0], pltpu.roll(gate[1], half, 1))
-    turned = split(jnp.transpose(packed))
-    cosines = dot3(turned, (dft[0], dft[1]))
-    sines = dot3(turned, (dft[2], dft[3]))
-    real = cosines[:half] - sines[half:]
-    imag = cosines[half:] + sines[:half]
-    loads[3].wait()
+    wire_a = value(0)
+    wire_b = value(1)
+    wire_c = value(2)
+    gate = times(times(times(value(3), wire_a), wire_b), wire_c)
+    gate = plus(gate, times(value(4), wire_a))
+    gate = plus(gate, times(value(5), wire_b))
+    gate = plus(gate, times(value(6), wire_c))
+    gate = plus(gate, value(7))
+    values = short_transform(slices(*gate), 1.0)
+    real = stacked([value[0] for value in values])
+    imag = stacked([value[1] for value in values])
+    real, imag = times((real, imag), (spin[0], spin[1]))
+    real, imag = lane_transform(real, imag, 1.0)
+    real, imag = times((real, imag), (twist[0], twist[1]))
     loads[4].wait()
-    real, imag = (real * spin[0] - imag * spin[1], real * spin[1] + imag * spin[0])
-    values = [
-        (real[at * fast_local : (at + 1) * fast_local], imag[at * fast_local : (at + 1) * fast_local])
-        for at in range(low_len)
-    ]
-    values = short_transform(values)
-    tails = members // low_len
-    breadth = side // tails
-    for at in range(low_len):
-        rows_at = slice(at * fast_local, (at + 1) * fast_local)
-        real, imag = values[at]
-        cosine = twist[0, rows_at]
-        sine = twist[1, rows_at]
-        out_real = real * cosine - imag * sine
-        out_imag = real * sine + imag * cosine
-        for part in range(tails):
-            lanes = slice(part * breadth, (part + 1) * breadth)
-            send_tail[at * tails + part, :fast_local] = out_real[:, lanes]
-            send_tail[at * tails + part, fast_local:] = out_imag[:, lanes]
+
+    breadth = side * low_len // members
+    lane_piece = side // members
+    tile_lanes = low_len * lane_piece
+    lanes = lax.broadcasted_iota(jnp.int32, (2 * fast_local, tile_lanes), 1)
+    for tile in range(side // tile_lanes):
+        span = slice(tile * tile_lanes, (tile + 1) * tile_lanes)
+        pieces = [
+            jnp.concatenate(
+                [
+                    real[at * fast_local : (at + 1) * fast_local, span],
+                    imag[at * fast_local : (at + 1) * fast_local, span],
+                ],
+                0,
+            )
+            for at in range(low_len)
+        ]
+        bit = low_len // 2
+        while bit:
+            keep = (lanes // (lane_piece * bit)) % 2 == 0
+            for at in range(low_len):
+                if at & bit == 0:
+                    first, second = pieces[at], pieces[at + bit]
+                    pieces[at] = jnp.where(keep, first, pltpu.roll(second, lane_piece * bit, 1))
+                    pieces[at + bit] = jnp.where(
+                        keep, pltpu.roll(first, tile_lanes - lane_piece * bit, 1), second
+                    )
+            bit //= 2
+        for at in range(low_len):
+            send_tail[tile * low_len + at] = pieces[at]
 
     def tail_copy(target, slot):
         return pltpu.make_async_remote_copy(
@@ -577,8 +602,11 @@
         tail_copy(source, source).wait_recv()
     flat = recv_tail[...].reshape(members * 2 * fast_local, breadth)
     result = dot3(split(jnp.transpose(flat)), (final[0], final[1]))
-    out_ref[0] = result[:, : rows * fast_len]
-    out_ref[1] = result[:, rows * fast_len :]
+    for at in range(low_len):
+        picked = result[at * lane_piece : (at + 1) * lane_piece]
+        rows_at = pl.ds(at, lane_piece, stride=low_len)
+        out_ref[0, rows_at] = picked[:, : rows * fast_len]
+        out_ref[1, rows_at] = picked[:, rows * fast_len :]
 
     for step in range(1, members):
         target = lax.rem(me + step, members)
@@ -599,14 +627,11 @@
 
 def fused_on_device(sizes, trace):
     side, fast_len, fast_local, rows, groups, _ = sizes
-    local_cols = trace.shape[0]
     low_len = side // fast_len
     half = low_len * fast_local
-    wide = 2 * half
     members = rows * groups
     tables = [jnp.asarray(table) for table in fused_tables(sizes)]
-    block = jnp.transpose(trace.reshape(local_cols, side, low_len, fast_local), (1, 0, 2, 3))
-    block = block.reshape(side, wide)
+    block = jnp.transpose(trace, (0, 2, 1))
     vmem = pltpu.VMEM
     bf16 = jnp.bfloat16
     f32 = jnp.float32
@@ -615,8 +640,7 @@
     return pl.pallas_call(
         partial(fused_kernel, sizes),
         out_shape=jax.ShapeDtypeStruct((2, breadth, rows * fast_len), f32),
-        in_specs=[pl.BlockSpec(memory_space=vmem)]
-        + [pl.BlockSpec(memory_space=pl.ANY)] * len(tables),
+        in_specs=[pl.BlockSpec(memory_space=pltpu.HBM)] * (1 + len(tables)),
         out_specs=pl.BlockSpec(memory_space=vmem),
         scratch_shapes=[
             vmem((4, side, side), bf16),
@@ -624,20 +648,18 @@
             vmem((2, side, side), f32),
             vmem((2, half, side), f32),
             vmem((2, members * 2 * fast_local, 2 * rows * fast_len), bf16),
-            vmem((rows, side, wide), f32),
-            vmem((rows, side, wide), f32),
-            vmem((8, wide), f32),
-            vmem((2 * side, side), bf16),
-            vmem((2 * side, side), bf16),
-            vmem((2 * side, side), bf16),
-            vmem((2 * side, side), bf16),
-            vmem((groups, side + 8, wide), f32),
-            vmem((groups, side + 8, wide), f32),
+            vmem((rows,) + block.shape, f32),
+            vmem((2, fast_local, side), f32),
+            vmem((side, 2 * side), bf16),
+            vmem((side, 2 * side), bf16),
+            vmem((2, side, side), f32),
+            vmem((groups, 2 * half + 8, side), f32),
+            vmem((groups, 2 * half + 8, side), f32),
             vmem((members, 2 * fast_local, breadth), f32),
             vmem((members, 2 * fast_local, breadth), f32),
             vmem((2, side, side), f32),
             vmem((2, half, side), f32),
-            dma((5,)),
+            dma((6,)),
             dma((rows, CHUNKS, 2)),
             dma((rows, CHUNKS)),
             dma((groups,)),
@@ -646,7 +668,7 @@
             dma((members,)),
         ],
         compiler_params=pltpu.CompilerParams(
-            collective_id=0, has_side_effects=True, vmem_limit_bytes=24 * 2**20
+            collective_id=0, has_side_effects=True, vmem_limit_bytes=67043328 - 288 * 1024
         ),
     )(block, *tables)
 

time: 35.7 us -> 31.3 us (0.88)
  local copies, waits for them, and re-layouts: 6.46 us -> 1.57 us
  Pallas kernels: 29 us -> 29.6 us
    reshape x2 -> x0, local copies, waits for them, and re-layouts: 3.64 us -> none  [the longest x1 3.53 us: fused_on_device(): trace.reshape(local_cols, side, low_len, fast_local)]
    transpose x1 -> x0, local copies, waits for them, and re-layouts: 2.15 us -> none  [fused_on_device(): jnp.transpose(trace.reshape(local_cols, side, low_len, fast_local), (1, 0...]
    unnamed x11 -> x1, local copies, waits for them, and re-layouts: 0.68 us -> 1.57 us
    pallas_call x1, Pallas kernels: 29 us -> 29.6 us  [fused_on_device(): pl.pallas_call(partial(fused_kernel, sizes), out_shape=jax.ShapeDtypeStru...]
where the time goes in v2:
time: 31.3 us; the launch traced here: 31.1 us
  Pallas kernels  29.6 us (95%)
  local copies, waits for them, and re-layouts  1.57 us (5%)
    pallas_call x1, Pallas kernels, fused_on_device(): pl.pallas_call(partial(fused_kernel, sizes), out_shape=jax.ShapeDtypeStru...  29.6 us
    unnamed x1, local copies, waits for them, and re-layouts  1.57 us

profile of v2, /device:TPU:0, one launch (start us, length us, event | category | flops | bytes accessed | tf_op | source)
XLA Modules:
  0.0 31.1 jit_solution(13666322465463584100)
XLA Ops:
  0.0 29.6 %shard_map.64 = f32[2,128,128]{2,1,0:T(8,128)} custom-call(f32[2,8,2048]{2,1,0:T(8,128)} %bitcast.1, bf16[4,256,256]{2,1,0:T(8,128)(2,1)} %constant.10.clone.dft_hbm, bf16[4,2,256,256]{3,2,1,0:T(8,128)(2,1)} %constant.11.clone.kern_hbm, f32[2,256,256]{2,1,0:T(8,128)} %constant.12.clone.base_hbm, f32[2,64,256]{2,1,0:T(8,128)} %constant.13.clone.spin_hbm, ...), custom_call_target="tpu_custom_call" | custom-call | tf_op jit(solution)/shard_map/pallas_call | solution.py:640
  29.6 1.6 %copy.8 = f32[2,128,128]{2,1,0:T(8,128)} copy(f32[2,128,128]{2,1,0:T(8,128)} %shard_map.64) | data formatting | bytes 262144

commit v3 on v2

--- a/solution.py
+++ b/solution.py
@@ -280,7 +280,6 @@
     total,
     data_high,
     data_low,
-    wide,
     send_block,
     recv_block,
     send_tail,
@@ -317,14 +316,8 @@
         }
 
     barrier = pltpu.get_barrier_semaphore()
-    for step in range(1, groups):
-        other = lax.rem(group + step, groups)
-        pl.semaphore_signal(
-            barrier,
-            inc=1,
-            device_id={"cols": lax.div(other, subs), "sub": lax.rem(other, subs)},
-            device_id_type=MESH,
-        )
+    for near in ({"cols": 1 - col}, {"sub": 1 - sub}):
+        pl.semaphore_signal(barrier, inc=1, device_id=near, device_id_type=MESH)
 
     @pl.when(row > 0)
     def _():
@@ -345,17 +338,28 @@
         load.start()
     pl.semaphore_wait(
         barrier,
-        groups - 1 + (row > 0).astype(jnp.int32) + (row < rows - 1).astype(jnp.int32),
-    )
-
-    def hop(source, slot, chunk, way, target):
+        2 + (row > 0).astype(jnp.int32) + (row < rows - 1).astype(jnp.int32),
+    )
+
+    def hop(source, slot, chunk, way, near):
         span = pl.ds(chunk * piece, piece)
         return pltpu.make_async_remote_copy(
             src_ref=source.at[:, :, span],
-            dst_ref=gathered.at[slot, :, :, span],
+            dst_ref=gathered.at[slot, col, :, :, span],
             send_sem=gather_send.at[slot, chunk, way],
-            recv_sem=gather_recv.at[slot, chunk],
-            device_id={"rows": target},
+            recv_sem=gather_recv.at[slot, col, chunk],
+            device_id=near,
+            device_id_type=MESH,
+        )
+
+    def across_arrival(slot, chunk):
+        span = pl.ds(chunk * piece, piece)
+        return pltpu.make_async_remote_copy(
+            src_ref=x_ref.at[:, :, span],
+            dst_ref=gathered.at[slot, 1 - col, :, :, span],
+            send_sem=gather_send.at[slot, chunk, 2],
+            recv_sem=gather_recv.at[slot, 1 - col, chunk],
+            device_id={"cols": 1 - col},
             device_id_type=MESH,
         )
 
@@ -363,13 +367,15 @@
 
         @pl.when(row < rows - 1)
         def _():
-            hop(x_ref, row, chunk, 0, row + 1).start()
+            hop(x_ref, row, chunk, 0, {"rows": row + 1}).start()
 
         @pl.when(row > 0)
         def _():
-            hop(x_ref, row, chunk, 1, row - 1).start()
-
-    own = pltpu.make_async_copy(x_ref, gathered.at[row], table_sem.at[5])
+            hop(x_ref, row, chunk, 1, {"rows": row - 1}).start()
+
+        hop(x_ref, row, chunk, 2, {"cols": 1 - col}).start()
+
+    own = pltpu.make_async_copy(x_ref, gathered.at[row, col], table_sem.at[5])
     own.start()
 
     def stacked(values):
@@ -391,11 +397,11 @@
             cosines[count:] + orient * sines[:count],
         )
 
-    def first_stage(slot):
+    def first_stage(slot, pair):
         values = [
             (
-                gathered[slot, 0, :, at * side : (at + 1) * side],
-                gathered[slot, 1, :, at * side : (at + 1) * side],
+                gathered[slot, pair, 0, :, at * side : (at + 1) * side],
+                gathered[slot, pair, 1, :, at * side : (at + 1) * side],
             )
             for at in range(low_len)
         ]
@@ -403,7 +409,7 @@
             sums = values[0][at]
             for value in values[1:]:
                 sums = sums + value[at]
-            total[at] += sums
+            total[pair, at] += sums
         values = short_transform(values, 1.0)
         real = stacked([value[0] for value in values])
         imag = stacked([value[1] for value in values])
@@ -412,11 +418,11 @@
         span = pl.ds(pl.multiple_of(slot * half, half), half)
         real, imag = times((real, imag), (base[0, span], base[1, span]))
         high, low = split(real)
-        data_high[span, :side] = high
-        data_low[span, :side] = low
+        data_high[pair, span, :side] = high
+        data_low[pair, span, :side] = low
         high, low = split(imag)
-        data_high[span, side:] = high
-        data_low[span, side:] = low
+        data_high[pair, span, side:] = high
+        data_low[pair, span, side:] = low
 
     shift = 0.5 / rows - row.astype(jnp.float32) / rows
     at_row = lax.broadcasted_iota(jnp.int32, (half, side), 0)
@@ -428,7 +434,7 @@
     loads[0].wait()
     loads[1].wait()
     loads[3].wait()
-    first_stage(row)
+    first_stage(row, col)
     centred = (low_freq - side * low_len // 2).astype(jnp.float32)
     angle = centred * (shift * (2.0 * math.pi / points))
     turn_cos = jnp.cos(angle)
@@ -441,91 +447,87 @@
     twist[0] = jnp.cos(tail_angle)
     twist[1] = jnp.sin(tail_angle)
 
-    @pl.loop(0, rows - 1)
+    def slot_of(step):
+        inner = jnp.where(
+            step == 1, row - 1, jnp.where(step == 2, row + 1, 2 * rows - 2 - 3 * row)
+        )
+        outer = jnp.where(row == 0, step, rows - 1 - step)
+        slot = jnp.where((row == 0) | (row == rows - 1), outer, inner)
+        return jnp.where(step == 0, row, slot)
+
+    @pl.loop(1, rows + 1)
     def _(step):
-        inner = jnp.where(
-            step == 0, row - 1, jnp.where(step == 1, row + 1, 2 * rows - 2 - 3 * row)
-        )
-        slot = jnp.where(
-            row == 0, step + 1, jnp.where(row == rows - 1, rows - 2 - step, inner)
-        )
+        @pl.when(step < rows)
+        def _():
+            slot = slot_of(step)
+            for chunk in range(CHUNKS):
+                hop(x_ref, slot, chunk, 0, {"cols": 1 - col}).wait_recv()
+
+                @pl.when((slot < row) & (row < rows - 1))
+                def _():
+                    hop(gathered.at[slot, col], slot, chunk, 0, {"rows": row + 1}).start()
+
+                @pl.when((slot > row) & (row > 0))
+                def _():
+                    hop(gathered.at[slot, col], slot, chunk, 1, {"rows": row - 1}).start()
+
+                hop(gathered.at[slot, col], slot, chunk, 2, {"cols": 1 - col}).start()
+            first_stage(slot, col)
+
+        before = slot_of(step - 1)
         for chunk in range(CHUNKS):
-            hop(x_ref, slot, chunk, 0, row).wait_recv()
-
-            @pl.when((slot < row) & (row < rows - 1))
-            def _():
-                hop(gathered.at[slot], slot, chunk, 0, row + 1).start()
-
-            @pl.when((slot > row) & (row > 0))
-            def _():
-                hop(gathered.at[slot], slot, chunk, 1, row - 1).start()
-
-        first_stage(slot)
-
-    mean_a = jnp.sum(jnp.sum(total[0], 0, keepdims=True), 1, keepdims=True) * (1.0 / points)
-    mean_b = jnp.sum(jnp.sum(total[1], 0, keepdims=True), 1, keepdims=True) * (1.0 / points)
-    loads[2].wait()
-    moved = dot3((kern[0], kern[1]), (data_high[...], data_low[...]))
-    real, imag = times((moved[:, :side], moved[:, side:]), (post[0], post[1]))
+            across_arrival(before, chunk).wait_recv()
+        first_stage(before, 1 - col)
+
     half_turn = jnp.zeros((1, 1), jnp.float32) + shift * math.pi
     half_cos = jnp.cos(half_turn)
     half_sin = jnp.sin(half_turn)
-    row_at = lax.broadcasted_iota(jnp.int32, (rows * half, side), 0)
-    lane_at = lax.broadcasted_iota(jnp.int32, (rows * half, side), 1)
+    mine = subs * half
+    row_at = lax.broadcasted_iota(jnp.int32, (mine, side), 0)
+    lane_at = lax.broadcasted_iota(jnp.int32, (mine, side), 1)
     constant = (lane_at == 0) & (row_at % half < fast_local)
     parity = jnp.where(constant, (1 - 2 * (row_at % 2)).astype(jnp.float32), 0.0)
-    wide[0] = real - parity * (mean_a * half_cos + mean_b * half_sin)
-    wide[1] = imag - parity * (mean_b * half_cos - mean_a * half_sin)
     side_at = lax.broadcasted_iota(jnp.int32, (8, side), 1)
-    means = jnp.where(side_at < side // 2, mean_a, mean_b)
-
-    def block_copy(target):
+    span = pl.ds(pl.multiple_of(col * mine, mine), mine)
+    loads[2].wait()
+
+    def block_copy(pair, origin):
         return pltpu.make_async_remote_copy(
-            src_ref=send_block.at[target],
-            dst_ref=recv_block.at[group],
-            send_sem=block_send.at[target],
-            recv_sem=block_recv.at[group],
-            device_id={"cols": lax.div(target, subs), "sub": lax.rem(target, subs)},
+            src_ref=send_block.at[pair, 1 - sub],
+            dst_ref=recv_block.at[pair * subs + origin],
+            send_sem=block_send.at[pair],
+            recv_sem=block_recv.at[pair * subs + origin],
+            device_id={"sub": 1 - sub},
             device_id_type=MESH,
         )
 
-    def block_arrival(source):
-        return pltpu.make_async_remote_copy(
-            src_ref=send_block.at[source],
-            dst_ref=recv_block.at[source],
-            send_sem=block_send.at[source],
-            recv_sem=block_recv.at[source],
-            device_id={"cols": lax.div(source, subs), "sub": lax.rem(source, subs)},
-            device_id_type=MESH,
-        )
-
-    @pl.loop(0, cols)
-    def _(step):
-        tile = lax.rem(col + 1 + step, cols)
-        span = pl.ds(pl.multiple_of(tile * subs * half, subs * half), subs * half)
-        real, imag = lane_transform(wide[0, span], wide[1, span], -1.0)
+    for pair in range(cols):
+        mean_a, mean_b = (
+            jnp.sum(jnp.sum(total[pair, at], 0, keepdims=True), 1, keepdims=True)
+            * (1.0 / points)
+            for at in range(2)
+        )
+        moved = dot3((kern[0, span], kern[1, span]), (data_high[pair], data_low[pair]))
+        real, imag = times((moved[:, :side], moved[:, side:]), (post[0, span], post[1, span]))
+        real = real - parity * (mean_a * half_cos + mean_b * half_sin)
+        imag = imag - parity * (mean_b * half_cos - mean_a * half_sin)
+        means = jnp.where(side_at < side // 2, mean_a, mean_b)
+        real, imag = lane_transform(real, imag, -1.0)
         for at in range(subs):
-            target = tile * subs + at
             values = times(
                 (real[at * half : (at + 1) * half], imag[at * half : (at + 1) * half]),
                 (spin[0], -spin[1]),
             )
             values = short_transform(slices(*values), -1.0)
             for low in range(low_len):
-                rows_at = slice(low * fast_local, (low + 1) * fast_local)
-                send_block[target, rows_at] = values[low][0]
-                send_block[target, half + low * fast_local : half + (low + 1) * fast_local] = (
-                    values[low][1]
-                )
-            send_block[target, 2 * half :] = means
-
-            @pl.when(target != group)
-            def _():
-                block_copy(target).start()
-
-    recv_block[group] = send_block[group]
-    for step in range(1, groups):
-        block_arrival(lax.rem(group + step, groups)).wait_recv()
+                for part in range(2):
+                    start = part * half + low * fast_local
+                    send_block[pair, at, start : start + fast_local] = values[low][part]
+            send_block[pair, at, 2 * half :] = means
+        block_copy(pair, sub).start()
+        recv_block[pair * subs + sub] = send_block[pair, sub]
+    for pair in range(cols):
+        block_copy(pair, 1 - sub).wait_recv()
 
     flip = (1 - 2 * (at_row % 2)).astype(jnp.float32)
     part_cos = flip * half_cos
@@ -611,22 +613,24 @@
     for step in range(1, members):
         target = lax.rem(me + step, members)
         tail_copy(target, me).wait_send()
-    for step in range(1, groups):
-        block_copy(lax.rem(group + step, groups)).wait_send()
+    for pair in range(cols):
+        block_copy(pair, sub).wait_send()
     for chunk in range(CHUNKS):
         for slot in range(rows):
 
             @pl.when((slot <= row) & (row < rows - 1))
             def _():
-                hop(x_ref, slot, chunk, 0, row + 1).wait_send()
+                hop(x_ref, slot, chunk, 0, {"rows": row + 1}).wait_send()
 
             @pl.when((slot >= row) & (row > 0))
             def _():
-                hop(x_ref, slot, chunk, 1, row - 1).wait_send()
+                hop(x_ref, slot, chunk, 1, {"rows": row - 1}).wait_send()
+
+            hop(x_ref, slot, chunk, 2, {"cols": 1 - col}).wait_send()
 
 
 def fused_on_device(sizes, trace):
-    side, fast_len, fast_local, rows, groups, _ = sizes
+    side, fast_len, fast_local, rows, groups, (cols, subs) = sizes
     low_len = side // fast_len
     half = low_len * fast_local
     members = rows * groups
@@ -648,21 +652,20 @@
             vmem((2, side, side), f32),
             vmem((2, half, side), f32),
             vmem((2, members * 2 * fast_local, 2 * rows * fast_len), bf16),
-            vmem((rows,) + block.shape, f32),
-            vmem((2, fast_local, side), f32),
-            vmem((side, 2 * side), bf16),
-            vmem((side, 2 * side), bf16),
-            vmem((2, side, side), f32),
-            vmem((groups, 2 * half + 8, side), f32),
+            vmem((rows, cols) + block.shape, f32),
+            vmem((cols, 2, fast_local, side), f32),
+            vmem((cols, side, 2 * side), bf16),
+            vmem((cols, side, 2 * side), bf16),
+            vmem((cols, subs, 2 * half + 8, side), f32),
             vmem((groups, 2 * half + 8, side), f32),
             vmem((members, 2 * fast_local, breadth), f32),
             vmem((members, 2 * fast_local, breadth), f32),
             vmem((2, side, side), f32),
             vmem((2, half, side), f32),
             dma((6,)),
-            dma((rows, CHUNKS, 2)),
-            dma((rows, CHUNKS)),
-            dma((groups,)),
+            dma((rows, CHUNKS, 3)),
+            dma((rows, cols, CHUNKS)),
+            dma((cols,)),
             dma((groups,)),
             dma((members,)),
             dma((members,)),

time: 31.3 us -> 31.3 us (level)
  no operation moved by 1% of the time
where the time goes in v3:
time: 31.3 us; the launch traced here: 31.2 us
  Pallas kernels  29.6 us (95%)
  local copies, waits for them, and re-layouts  1.57 us (5%)
    pallas_call x1, Pallas kernels, fused_on_device(): pl.pallas_call(partial(fused_kernel, sizes), out_shape=jax.ShapeDtypeStru...  29.6 us
    unnamed x1, local copies, waits for them, and re-layouts  1.57 us

profile of v3, /device:TPU:0, one launch (start us, length us, event | category | flops | bytes accessed | tf_op | source)
XLA Modules:
  0.0 31.2 jit_solution(480697470701878970)
XLA Ops:
  0.0 29.6 %shard_map.64 = f32[2,128,128]{2,1,0:T(8,128)} custom-call(f32[2,8,2048]{2,1,0:T(8,128)} %bitcast.1, bf16[4,256,256]{2,1,0:T(8,128)(2,1)} %constant.10.clone.dft_hbm, bf16[4,2,256,256]{3,2,1,0:T(8,128)(2,1)} %constant.11.clone.kern_hbm, f32[2,256,256]{2,1,0:T(8,128)} %constant.12.clone.base_hbm, f32[2,64,256]{2,1,0:T(8,128)} %constant.13.clone.spin_hbm, ...), custom_call_target="tpu_custom_call" | custom-call | tf_op jit(solution)/shard_map/pallas_call | solution.py:644
  29.6 1.6 %copy.8 = f32[2,128,128]{2,1,0:T(8,128)} copy(f32[2,128,128]{2,1,0:T(8,128)} %shard_map.64) | data formatting | bytes 262144

commit v4 on v3

--- a/solution.py
+++ b/solution.py
@@ -429,12 +429,50 @@
     at_lane = lax.broadcasted_iota(jnp.int32, (half, side), 1)
     low_freq = at_row // fast_local + low_len * at_lane
     digit = rows * (fast_local * group + at_row % fast_local) + row
+    inner = (row > 0) & (row < rows - 1)
+    first = jnp.where(row == 0, 1, jnp.where(row == rows - 1, rows - 2, rows - 1 - row))
+    end = jnp.where(2 * row < rows, 0, rows - 1)
+    far = rows - 1 - end
+    near_far = jnp.where(end == 0, rows - 2, 1)
+    second = jnp.where(inner, far, near_far)
+    third = jnp.where(inner, end, far)
+
+    def relay(slot, chunk):
+        hop(x_ref, slot, chunk, 0, {"cols": 1 - col}).wait_recv()
+
+        @pl.when((slot < row) & (row < rows - 1))
+        def _():
+            hop(gathered.at[slot, col], slot, chunk, 0, {"rows": row + 1}).start()
+
+        @pl.when((slot > row) & (row > 0))
+        def _():
+            hop(gathered.at[slot, col], slot, chunk, 1, {"rows": row - 1}).start()
+
+        hop(gathered.at[slot, col], slot, chunk, 2, {"cols": 1 - col}).start()
+
+    def relay_near(chunk):
+        relay(first, chunk)
+
+        @pl.when(inner)
+        def _():
+            relay(third, chunk)
+
+    def across(slot):
+        for chunk in range(CHUNKS):
+            across_arrival(slot, chunk).wait_recv()
+        first_stage(slot, 1 - col)
+
     total[...] = jnp.zeros_like(total)
     own.wait()
     loads[0].wait()
     loads[1].wait()
     loads[3].wait()
+    middle = CHUNKS // 2
+    for chunk in range(middle):
+        relay_near(chunk)
     first_stage(row, col)
+    for chunk in range(middle, CHUNKS):
+        relay_near(chunk)
     centred = (low_freq - side * low_len // 2).astype(jnp.float32)
     angle = centred * (shift * (2.0 * math.pi / points))
     turn_cos = jnp.cos(angle)
@@ -443,41 +481,26 @@
         span = slice(at * half, (at + 1) * half)
         post[0, span] = base[0, span] * turn_cos + base[1, span] * turn_sin
         post[1, span] = base[0, span] * turn_sin - base[1, span] * turn_cos
+    for chunk in range(middle):
+        relay(second, chunk)
     tail_angle = ((low_freq * (2 * digit - 1)) % (2 * ext)).astype(jnp.float32) * (math.pi / ext)
     twist[0] = jnp.cos(tail_angle)
     twist[1] = jnp.sin(tail_angle)
-
-    def slot_of(step):
-        inner = jnp.where(
-            step == 1, row - 1, jnp.where(step == 2, row + 1, 2 * rows - 2 - 3 * row)
-        )
-        outer = jnp.where(row == 0, step, rows - 1 - step)
-        slot = jnp.where((row == 0) | (row == rows - 1), outer, inner)
-        return jnp.where(step == 0, row, slot)
-
-    @pl.loop(1, rows + 1)
-    def _(step):
-        @pl.when(step < rows)
+    for chunk in range(middle, CHUNKS):
+        relay(second, chunk)
+    first_stage(first, col)
+    across(row)
+    for chunk in range(CHUNKS):
+
+        @pl.when(jnp.logical_not(inner))
         def _():
-            slot = slot_of(step)
-            for chunk in range(CHUNKS):
-                hop(x_ref, slot, chunk, 0, {"cols": 1 - col}).wait_recv()
-
-                @pl.when((slot < row) & (row < rows - 1))
-                def _():
-                    hop(gathered.at[slot, col], slot, chunk, 0, {"rows": row + 1}).start()
-
-                @pl.when((slot > row) & (row > 0))
-                def _():
-                    hop(gathered.at[slot, col], slot, chunk, 1, {"rows": row - 1}).start()
-
-                hop(gathered.at[slot, col], slot, chunk, 2, {"cols": 1 - col}).start()
-            first_stage(slot, col)
-
-        before = slot_of(step - 1)
-        for chunk in range(CHUNKS):
-            across_arrival(before, chunk).wait_recv()
-        first_stage(before, 1 - col)
+            relay(third, chunk)
+
+    first_stage(second, col)
+    across(first)
+    first_stage(third, col)
+    across(second)
+    across(third)
 
     half_turn = jnp.zeros((1, 1), jnp.float32) + shift * math.pi
     half_cos = jnp.cos(half_turn)

time: 31.3 us -> 29.4 us (0.939)
  Pallas kernels: 29.6 us -> 27.7 us
    pallas_call x1, Pallas kernels: 29.6 us -> 27.7 us  [fused_on_device(): pl.pallas_call(partial(fused_kernel, sizes), out_shape=jax.ShapeDtypeStru...]
where the time goes in v4:
time: 29.4 us; the launch traced here: 29.2 us
  Pallas kernels  27.7 us (94%)
  local copies, waits for them, and re-layouts  1.57 us (5%)
    pallas_call x1, Pallas kernels, fused_on_device(): pl.pallas_call(partial(fused_kernel, sizes), out_shape=jax.ShapeDtypeStru...  27.7 us
    unnamed x1, local copies, waits for them, and re-layouts  1.57 us

profile of v4, /device:TPU:0, one launch (start us, length us, event | category | flops | bytes accessed | tf_op | source)
XLA Modules:
  0.0 29.2 jit_solution(3393411554103253357)
XLA Ops:
  0.0 27.7 %shard_map.64 = f32[2,128,128]{2,1,0:T(8,128)} custom-call(f32[2,8,2048]{2,1,0:T(8,128)} %bitcast.1, bf16[4,256,256]{2,1,0:T(8,128)(2,1)} %constant.10.clone.dft_hbm, bf16[4,2,256,256]{3,2,1,0:T(8,128)(2,1)} %constant.11.clone.kern_hbm, f32[2,256,256]{2,1,0:T(8,128)} %constant.12.clone.base_hbm, f32[2,64,256]{2,1,0:T(8,128)} %constant.13.clone.spin_hbm, ...), custom_call_target="tpu_custom_call" | custom-call | tf_op jit(solution)/shard_map/pallas_call | solution.py:667
  27.7 1.6 %copy.8 = f32[2,128,128]{2,1,0:T(8,128)} copy(f32[2,128,128]{2,1,0:T(8,128)} %shard_map.64) | data formatting | bytes 262144
